TPU v7x, 32 devices: a whole 2x2x4 slice. The times are simulated.
32 devices in a mesh: dp: 2 (over x), fsdp: 4 (over z), expert: 4 (over y, core).
Axes of the slice: x: 2, y: 2, z: 4, core: 2. Of those that a mesh axis runs over, the one named last changes fastest.
Arguments:
- window: bfloat16 [256, 4096], P('fsdp'), may hold values from -3 to 3
- attention_gain: float32 [4096], replicated, may hold values from 0.1 to 1.9
- query_weight: bfloat16 [4096, 4096], P('fsdp', 'expert'), may hold values from -0.09375 to 0.09375
- key_weight: bfloat16 [4096, 1024], P('fsdp', 'expert'), may hold values from -0.1875 to 0.1875
- value_weight: bfloat16 [4096, 1024], P('fsdp', 'expert'), may hold values from -0.1875 to 0.1875
- out_weight: bfloat16 [4096, 4096], P('expert', 'fsdp'), may hold values from -0.1875 to 0.1875
- cache_keys: bfloat16 [1024, 1024], P('dp', 'expert'), may hold values from -104 to 104
- cache_values: bfloat16 [1024, 1024], P('dp', 'expert'), may hold values from -12 to 12
- occluded: int32 [1024, 2], P('dp'), may hold values from 0 to 1, as said below
- feedforward_gain: float32 [4096], replicated, may hold values from 0.1 to 1.9
- router_weight: bfloat16 [4096, 4], replicated, may hold values from -0.0234375 to 0.0234375
- chosen_experts: int32 [2, 256, 2], P('dp', 'fsdp'), may hold values from 0 to 3, all different within a row; in each aligned block of 64 rows (0 to 63, 64 to 127, ..., all dimensions but the last counted through in order) at most 64 rows name the same one
- gate_weight: bfloat16 [4, 12288, 4096], P('expert', ('dp', 'fsdp')), may hold values from -0.09375 to 0.09375
- up_weight: bfloat16 [4, 12288, 4096], P('expert', ('dp', 'fsdp')), may hold values from -0.09375 to 0.09375
- down_weight: bfloat16 [4, 12288, 4096], P('expert', ('dp', 'fsdp')), may hold values from -0.0546875 to 0.0546875
Outputs:
- layer_output: bfloat16 [2, 256, 4096], P('dp', 'fsdp')
Inputs may be any that keep to these rules, and one draw needn't show every extreme that they name: `chosen_experts`: each row names 2 different experts. In each aligned block of 64 rows, counting the leading dimensions together (the rows of one device), no expert is named by more than 64 rows, a bound that some block reaches. `occluded`: constant over each aligned run of 64 prefix positions.
All inputs are finite; a program needn't handle non-finite values.
Results may differ from a plain program's by a relative error of at most 0.0095.
The roundings to bfloat16 on the way count: a program that leaves them out, or rounds other values in their place, can miss the bound.
Values may be sent and summed in bfloat16 or wider, within the bound.
A program may use at most 128 MiB of HBM per device.

v0:
```python
import jax
import jax.numpy as jnp
from jax import lax
from jax.sharding import PartitionSpec as P

HD = 128
TOP = 2
epsilon = 1e-05
rope_base = 1000000.0
floor_score = -1e30


def rms_norm(values, scales):
    widened = values.astype(jnp.float32)
    inverse = lax.rsqrt(jnp.mean(widened * widened, axis=-1, keepdims=True) + epsilon)
    return (widened * inverse * scales).astype(jnp.bfloat16)


def rotate(vectors, positions):
    halfway = vectors.shape[-1] // 2
    powers = jnp.arange(halfway, dtype=jnp.float32) * (2.0 / vectors.shape[-1])
    frequency = rope_base ** (-powers)
    angles = positions.astype(jnp.float32)[:, None] * frequency[None, :]
    cosine = jnp.cos(angles)[:, None, :]
    sine_part = jnp.sin(angles)[:, None, :]
    former = vectors[..., :halfway]
    latter = vectors[..., halfway:]
    return jnp.concatenate(
        [former * cosine - latter * sine_part, latter * cosine + former * sine_part], axis=-1
    )


def absorb_block(running, scores, visible, values_block):
    running_top, running_total, running_output = running
    masked = jnp.where(visible, scores, floor_score)
    fresh_top = jnp.maximum(running_top, jnp.max(masked, axis=-1))
    weights = jnp.where(visible, jnp.exp(masked - fresh_top[..., None]), 0.0)
    fresh_total = jnp.sum(weights, axis=-1)
    fresh_output = jnp.einsum(
        "kgtn,nkd->kgtd",
        weights.astype(jnp.bfloat16),
        values_block,
        preferred_element_type=jnp.float32,
    )
    return (fresh_top, fresh_total, fresh_output)


def local(
    window,
    attention_gain,
    query_weight,
    key_weight,
    value_weight,
    out_weight,
    cache_keys,
    cache_values,
    occluded,
    feedforward_gain,
    router_weight,
    chosen_experts,
    gate_weight,
    up_weight,
    down_weight,
):
    token_rows = window.shape[0]
    fsdp_count = lax.axis_size("fsdp")
    fsdp_place = lax.axis_index("fsdp")
    data_place = lax.axis_index("dp")
    expert_place = lax.axis_index("expert")
    query_heads = query_weight.shape[1] // HD
    key_heads = key_weight.shape[1] // HD
    grouping = query_heads // key_heads
    window_rows = token_rows * fsdp_count
    prefix_rows = cache_keys.shape[0] * lax.axis_size("dp")
    score_scale = HD ** (-0.5)
    normed = rms_norm(window, attention_gain)
    first_row = fsdp_place * token_rows
    own_positions = prefix_rows + first_row + jnp.arange(token_rows, dtype=jnp.int32)
    all_positions = prefix_rows + jnp.arange(window_rows, dtype=jnp.int32)
    everyone = lax.all_gather(normed, "fsdp", axis=0, tiled=True)
    slab_width = query_weight.shape[0]
    columns = lax.dynamic_slice_in_dim(everyone, fsdp_place * slab_width, slab_width, 1)
    row_block = columns
    query_sum = lax.psum_scatter(
        jnp.dot(row_block, query_weight, preferred_element_type=jnp.float32),
        "fsdp",
        scatter_dimension=0,
        tiled=True,
    )
    key_sum, value_sum = lax.psum(
        (
            jnp.dot(columns, key_weight, preferred_element_type=jnp.float32),
            jnp.dot(columns, value_weight, preferred_element_type=jnp.float32),
        ),
        "fsdp",
    )
    queries = rotate(query_sum.reshape(token_rows, query_heads, HD), own_positions).astype(
        jnp.bfloat16
    )
    window_keys = (
        rotate(key_sum.reshape(window_rows, key_heads, HD), all_positions)
        .astype(jnp.bfloat16)
        .reshape(window_rows, key_heads * HD)
    )
    window_values = value_sum.astype(jnp.bfloat16)
    query_grid = queries.reshape(token_rows, key_heads, grouping, HD)
    fresh_keys = window_keys.reshape(window_rows, key_heads, HD)
    fresh_values = window_values.reshape(window_rows, key_heads, HD)
    window_scores = (
        jnp.einsum("tkgd,nkd->kgtn", query_grid, fresh_keys, preferred_element_type=jnp.float32)
        * score_scale
    )
    causal = jnp.arange(window_rows)[None, :] <= (first_row + jnp.arange(token_rows))[:, None]
    empty_state = (
        jnp.full((key_heads, grouping, token_rows), floor_score, jnp.float32),
        jnp.zeros((key_heads, grouping, token_rows), jnp.float32),
        jnp.zeros((key_heads, grouping, token_rows, HD), jnp.float32),
    )
    window_state = absorb_block(empty_state, window_scores, causal, fresh_values)
    occluded_flags = occluded.astype(jnp.bfloat16)
    keys_block = lax.all_gather(cache_keys, "dp", axis=0, tiled=True)
    values_block = lax.all_gather(cache_values, "dp", axis=0, tiled=True)
    flags_block = lax.all_gather(occluded_flags, "dp", axis=0, tiled=True)
    block_length = keys_block.shape[0]
    scores = (
        jnp.einsum(
            "tkgd,nkd->kgtn",
            query_grid,
            keys_block.reshape(block_length, key_heads, HD),
            preferred_element_type=jnp.float32,
        )
        * score_scale
    )
    visible = lax.dynamic_slice_in_dim(flags_block, data_place, 1, 1)[:, 0] == 0
    prefix_state = absorb_block(
        empty_state, scores, visible, values_block.reshape(block_length, key_heads, HD)
    )
    overall = jnp.maximum(prefix_state[0], window_state[0])
    prefix_fade = jnp.exp(prefix_state[0] - overall)
    window_fade = jnp.exp(window_state[0] - overall)
    denominator = prefix_state[1] * prefix_fade + window_state[1] * window_fade
    head_values = (
        prefix_state[2] * prefix_fade[..., None] + window_state[2] * window_fade[..., None]
    ) / denominator[..., None]
    attended = (
        head_values.transpose(2, 0, 1, 3).reshape(token_rows, query_heads * HD).astype(jnp.bfloat16)
    )
    head_terms = jnp.dot(
        attended,
        lax.all_gather(out_weight, "fsdp", axis=1, tiled=True),
        preferred_element_type=jnp.float32,
    )
    residual = window.astype(jnp.float32) + lax.psum(head_terms, "expert")
    normed_mix = rms_norm(residual, feedforward_gain)
    logits = jnp.dot(normed_mix, router_weight, preferred_element_type=jnp.float32)
    expert_count = router_weight.shape[1]
    expert_picks = chosen_experts.reshape(token_rows, TOP)
    matches = expert_picks[:, :, None] == jnp.arange(expert_count, dtype=jnp.int32)[None, None, :]
    picked = jnp.sum(jnp.where(matches, logits[:, None, :], 0.0), axis=-1)
    gate_shares = jax.nn.sigmoid(picked - picked[:, ::-1])
    expert_hits = expert_picks == expert_place
    taken_flag = jnp.any(expert_hits, axis=1).astype(jnp.int32)
    weight_mine = jnp.sum(jnp.where(expert_hits, gate_shares, 0.0), axis=1)
    capacity = min(token_rows, 2 * token_rows * TOP // expert_count)
    slot_numbers = jnp.cumsum(taken_flag) - taken_flag
    placing = (slot_numbers[:, None] == jnp.arange(capacity, dtype=jnp.int32)[None, :]) & (
        taken_flag[:, None] == 1
    )
    send_rows = lax.dot_general(
        placing.astype(jnp.bfloat16),
        normed_mix,
        (((0,), (0,)), ((), ())),
        preferred_element_type=jnp.float32,
    ).astype(jnp.bfloat16)
    gate_rows = gate_weight[0]
    up_rows = up_weight[0]
    down_rows = down_weight[0]
    contract_last = (((1,), (1,)), ((), ()))
    piece_rows = lax.all_gather(send_rows, ("dp", "fsdp"), axis=0, tiled=True)
    gate_values = lax.dot_general(
        piece_rows, gate_rows, contract_last, preferred_element_type=jnp.float32
    )
    lifted = lax.dot_general(piece_rows, up_rows, contract_last, preferred_element_type=jnp.float32)
    hidden = (jax.nn.silu(gate_values) * lifted).astype(jnp.bfloat16)
    row_block = hidden
    expert_output = lax.psum_scatter(
        jnp.dot(row_block, down_rows, preferred_element_type=jnp.float32).astype(jnp.bfloat16),
        ("dp", "fsdp"),
        scatter_dimension=0,
        tiled=True,
    ).astype(jnp.float32)
    returned = jnp.dot(
        placing.astype(jnp.float32),
        expert_output,
        precision=lax.Precision.HIGHEST,
        preferred_element_type=jnp.float32,
    )
    mixture = lax.psum(returned * weight_mine[:, None], "expert")
    return (residual + mixture).astype(jnp.bfloat16).reshape(1, token_rows, residual.shape[1])


def solution(mesh):
    placed = (
        P("fsdp", None),
        P(),
        P("fsdp", "expert"),
        P("fsdp", "expert"),
        P("fsdp", "expert"),
        P("expert", "fsdp"),
        P("dp", "expert"),
        P("dp", "expert"),
        P("dp", None),
        P(),
        P(),
        P("dp", "fsdp", None),
        P("expert", ("dp", "fsdp"), None),
        P("expert", ("dp", "fsdp"), None),
        P("expert", ("dp", "fsdp"), None),
    )
    return jax.shard_map(
        local, mesh=mesh, in_specs=placed, out_specs=P("dp", "fsdp", None), check_vma=False
    )
```

profile of v0, /device:TPU:0, one launch (start us, length us, event | category | flops | bytes accessed | tf_op | source)
XLA Modules:
  0.0 560.7 jit_solution(14526967308801473713)
XLA Ops:
  6.5 1.4 fusion.29
  8.0 2.0 fusion.31
  10.1 48.7 %all-gather.4.cloned.1.call-done = bf16[256,4096]{1,0:T(8,128)(2,1)} async-done(((bf16[64,4096]{1,0:T(8,128)(2,1)}), bf16[256,4096]{1,0:T(8,128)(2,1)}) %all-gather.4.cloned.1.call-update) | async-done | bytes 2097168 | tf_op jit(solution)/shard_map/all_gather | solution.py:80
  58.8 1.4 fusion.43
  60.2 0.8 copy.41
  61.1 2.7 fusion.45
  63.9 0.5 all-gather.6.cloned.1.call-update
  65.1 4.3 all_gather.18
  69.5 7.9 %all_gather.20 = bf16[1024,256]{0,1:T(8,128)(2,1)S(1)} all-gather(bf16[512,256]{0,1:T(8,128)(2,1)S(1)} %copy.37), channel_id=1, replica_groups=mesh['dp'=2,'fsdp'=4,'expert'=4] {'dp'}, dimensions={0}, use_global_device_ids=true | all-gather | bytes 786432 | tf_op jit(solution)/shard_map/all_gather | solution.py:121
  77.4 7.1 %all_gather.21 = bf16[1024,256]{0,1:T(8,128)(2,1)S(1)} all-gather(bf16[512,256]{0,1:T(8,128)(2,1)S(1)} %copy.39), channel_id=1, replica_groups=mesh['dp'=2,'fsdp'=4,'expert'=4] {'dp'}, dimensions={0}, use_global_device_ids=true | all-gather | bytes 786432 | tf_op jit(solution)/shard_map/all_gather | solution.py:122
  84.8 0.5 multiply_cosine_fusion
  85.3 1.3 fusion.41
  86.7 23.1 %all-reduce.10 = bf16[256,256]{1,0:T(8,128)(2,1)S(1)} all-reduce(f32[256,256]{1,0:T(8,128)S(1)} %fusion.41), channel_id=1, replica_groups=mesh['dp'=2,'fsdp'=4,'expert'=4] {'fsdp'}, use_global_device_ids=true, to_apply=%region_5.6 | all-reduce | flops 65536 | bytes 393216 | tf_op jit(solution)/shard_map/psum | solution.py:90
  109.9 1.2 subtract_convert_fusion
  111.1 14.3 %reduce-scatter.3.cloned.1.call-done = f32[64,1024]{1,0:T(8,128)} async-done(((f32[256,1024]{1,0:T(8,128)}), f32[64,1024]{1,0:T(8,128)}) %reduce-scatter.3.cloned.1.call-update) | async-done | bytes 262160 | tf_op jit(solution)/shard_map/reduce_scatter | solution.py:84
  125.4 1.0 copy.55
  127.3 0.6 bitcast_reduce_fusion
  127.9 0.6 fusion.20
  128.6 0.6 fusion.27
  129.8 145.4 %all-gather.6.cloned.1.call-done = bf16[1024,4096]{1,0:T(8,128)(2,1)} async-done(((bf16[1024,1024]{1,0:T(8,128)(2,1)}), bf16[1024,4096]{1,0:T(8,128)(2,1)}) %all-gather.6.cloned.1.call-update) | async-done | bytes 8388624 | tf_op jit(solution)/shard_map/all_gather | solution.py:150
  275.1 6.0 %fusion.80 = f32[64,4096]{1,0:T(8,128)} fusion(bf16[64,1024]{1,0:T(8,128)(2,1)S(1)} %convert_element_type.96, bf16[1024,4096]{1,0:T(8,128)(2,1)} %all-gather.6.cloned.1.call-done), kind=kOutput, calls=%fused_computation.113 | convolution fusion | flops 536870912 | bytes 9568256 | tf_op jit(solution)/shard_map/dot_general | solution.py:148
  281.6 34.0 %all-reduce.7.cloned.1.call-done = f32[64,4096]{1,0:T(8,128)} async-done(((f32[64,4096]{1,0:T(8,128)}), f32[64,4096]{1,0:T(8,128)}) %all-reduce.7.cloned.1.call-update) | async-done | bytes 1048592 | tf_op jit(solution)/shard_map/psum | solution.py:153
  315.6 1.6 multiply_reduce_fusion
  317.4 1.2 convolution_convert_fusion
  318.9 73.7 %all-gather.8.cloned.1.call-done = bf16[512,4096]{1,0:T(8,128)(2,1)} async-done(((bf16[64,4096]{1,0:T(8,128)(2,1)}), bf16[512,4096]{1,0:T(8,128)(2,1)}) %all-gather.8.cloned.1.call-update) | async-done | bytes 4194320 | tf_op jit(solution)/shard_map/all_gather | solution.py:179
  392.6 12.1 %fusion.4 = f32[512,1536]{1,0:T(8,128)} fusion(bf16[512,4096]{1,0:T(8,128)(2,1)} %all-gather.8.cloned.1.call-done, bf16[1,1536,4096]{2,1,0:T(8,128)(2,1)} %param.27), kind=kOutput, calls=%fused_computation.4 | convolution fusion | flops 6442450944 | bytes 19922944 | tf_op jit(solution)/shard_map/dot_general | solution.py:180
  404.7 21.8 %fusion.6 = bf16[512,4096]{1,0:T(8,128)(2,1)} fusion(bf16[1,1536,4096]{2,1,0:T(8,128)(2,1)} %param.29, bf16[512,4096]{1,0:T(8,128)(2,1)} %all-gather.8.cloned.1.call-done, bf16[1,1536,4096]{2,1,0:T(8,128)(2,1)} %param.28, f32[512,1536]{1,0:T(8,128)} %fusion.4), kind=kOutput, calls=%fused_computation.6 | convolution fusion | flops 12891717632 | bytes 36700160 | tf_op jit(solution)/shard_map/dot_general | solution.py:187
  426.6 0.7 copy-done.8
  427.6 85.3 %reduce-scatter.5.cloned.1.call-done = bf16[64,4096]{1,0:T(8,128)(2,1)} async-done(((bf16[512,4096]{1,0:T(8,128)(2,1)}), bf16[64,4096]{1,0:T(8,128)(2,1)}) %reduce-scatter.5.cloned.1.call-update) | async-done | bytes 524304 | tf_op jit(solution)/shard_map/reduce_scatter | solution.py:186
  512.9 2.4 convolution_multiply_fusion
  515.4 36.0 %all-reduce.9.cloned.1.call-done = f32[64,4096]{1,0:T(8,128)} async-done(((f32[64,4096]{1,0:T(8,128)}), f32[64,4096]{1,0:T(8,128)}) %all-reduce.9.cloned.1.call-update) | async-done | bytes 1048592 | tf_op jit(solution)/shard_map/psum | solution.py:198
  551.3 2.5 fusion.38
  (74 shorter events, 3.8 us)
Async XLA Ops:
  6.5 54.6 %copy-start = (bf16[1024,1024]{1,0:T(8,128)(2,1)S(1)}, bf16[1024,1024]{1,0:T(8,128)(2,1)}, u32[]{:S(2)}) copy-start(bf16[1024,1024]{1,0:T(8,128)(2,1)} %param.17) | copy-start | bytes 6291460
  6.5 52.3 %copy-start.4 = (bf16[1024,256]{1,0:T(8,128)(2,1)S(1)}, bf16[1024,256]{1,0:T(8,128)(2,1)}, u32[]{:S(2)}) copy-start(bf16[1024,256]{1,0:T(8,128)(2,1)} %param.18) | copy-start | bytes 1572868
  6.5 52.3 %all-gather.4.cloned.1.call-start = ((), (), s32[]{:S(2)}) async-start(), calls=%async_computation.2 | async-start | bytes 2621440 | tf_op jit(solution)/shard_map/all_gather | solution.py:80
  10.0 99.9 %all-reduce.5.cloned.1.call-start = ((), (), s32[]{:S(2)}) async-start(), calls=%async_computation.4 | async-start | bytes 524288 | tf_op jit(solution)/shard_map/psum | solution.py:90
  61.1 64.4 %reduce-scatter.3.cloned.1.call-start = ((), (), s32[]{:S(2)}) async-start(), calls=%async_computation.3 | async-start | bytes 1310720 | tf_op jit(solution)/shard_map/reduce_scatter | solution.py:84
  63.9 0.7 copy-start.11
  63.9 1.0 copy-start.6
  63.9 1.1 copy-start.7
  63.9 21.4 %copy-start.5 = (bf16[1024,256]{1,0:T(8,128)(2,1)S(1)}, bf16[1024,256]{1,0:T(8,128)(2,1)}, u32[]{:S(2)}) copy-start(bf16[1024,256]{1,0:T(8,128)(2,1)} %param.19) | copy-start | bytes 1572868
  63.9 211.2 %all-gather.6.cloned.1.call-start = ((), (), s32[]{:S(2)}) async-start(), calls=%async_computation.5 | async-start | bytes 10485760 | tf_op jit(solution)/shard_map/all_gather | solution.py:150
  64.5 251.1 %all-reduce.7.cloned.1.call-start = ((), (), s32[]{:S(2)}) async-start(), calls=%async_computation.6 | async-start | bytes 2097152 | tf_op jit(solution)/shard_map/psum | solution.py:153
  129.7 151.5 %copy-start.10 = (s32[1,64,2]{1,2,0:T(2,128)S(1)}, s32[1,64,2]{1,2,0:T(2,128)}, u32[]{:S(2)}) copy-start(s32[1,64,2]{1,2,0:T(2,128)} %param.26) | copy-start | bytes 1540
  129.7 185.9 %copy-start.2 = (bf16[64,4096]{1,0:T(8,128)(2,1)S(1)}, bf16[64,4096]{1,0:T(8,128)(2,1)}, u32[]{:S(2)}) copy-start(bf16[64,4096]{1,0:T(8,128)(2,1)} %param.15) | copy-start | bytes 1572868
  281.2 36.0 %copy-start.9 = (f32[4096]{0:T(1024)S(1)}, f32[4096]{0:T(1024)}, u32[]{:S(2)}) copy-start(f32[4096]{0:T(1024)} %param.24) | copy-start | bytes 49156
  281.2 111.4 %all-gather.8.cloned.1.call-start = ((), (), s32[]{:S(2)}) async-start(), calls=%async_computation.7 | async-start | bytes 4718592 | tf_op jit(solution)/shard_map/all_gather | solution.py:179
  315.6 1.6 copy-start.3
  318.7 194.2 %reduce-scatter.5.cloned.1.call-start = ((), (), s32[]{:S(2)}) async-start(), calls=%async_computation.8 | async-start | bytes 4718592 | tf_op jit(solution)/shard_map/reduce_scatter | solution.py:186
  426.5 0.8 copy-start.8
  426.5 124.8 %all-reduce.9.cloned.1.call-start = ((), (), s32[]{:S(2)}) async-start(), calls=%async_computation.9 | async-start | bytes 2097152 | tf_op jit(solution)/shard_map/psum | solution.py:198
  515.3 38.5 %copy-start.1 = (bf16[1024,1024]{1,0:T(8,128)(2,1)S(1)}, bf16[1024,1024]{1,0:T(8,128)(2,1)}, u32[]{:S(2)}) copy-start(bf16[1024,1024]{1,0:T(8,128)(2,1)} %param.17) | copy-start | bytes 6291460
Sparse Core Ops, SparseCore 0:
  10.1 48.6 all-gather.3
  61.2 34.6 all-reduce.4
  98.2 27.1 reduce-scatter.2
  126.8 148.2 all-gather.5
  281.3 34.2 all-reduce.6
  318.8 73.7 all-gather.7
  426.7 86.1 reduce-scatter.4
  515.5 35.8 all-reduce.8
where the time goes:
time: 561 us
  waiting for transfers between devices  438 us (78%)
  matrix products  51.2 us (9%)
  blocking collectives  42.4 us (8%)
  between operations  13.8 us (2%)
  other arithmetic  11.1 us (2%)
    all_gather x1, waiting for transfers between devices, local(): lax.all_gather(out_weight, 'fsdp', axis=1, tiled=True)  145 us
    reduce_scatter x1, waiting for transfers between devices, local(): lax.psum_scatter(jnp.dot(row_block, down_rows, preferred_element_type=jnp...  85.3 us
    all_gather x1, waiting for transfers between devices, local(): piece_rows = lax.all_gather(send_rows, ('dp', 'fsdp'), axis=0, tiled=True)  73.7 us
    all_gather x1, waiting for transfers between devices, local(): everyone = lax.all_gather(normed, 'fsdp', axis=0, tiled=True)  48.7 us
    psum x1, waiting for transfers between devices, local(): mixture = lax.psum(returned * weight_mine[:, None], 'expert')  36 us
    psum x1, waiting for transfers between devices, local(): residual = window.astype(jnp.float32) + lax.psum(head_terms, 'expert')  34 us
    psum x1, blocking collectives, local(): lax.psum((jnp.dot(columns, key_weight, preferred_element_type=jnp.float32...  23.1 us
    dot_general x1, matrix products, local(): jnp.dot(row_block, down_rows, preferred_element_type=jnp.float32)  21.8 us
  transfers between devices with their start and end apart: 8, of which 7 were waited for; matrix products, arithmetic and copies ran while one was open for 2% of the time, Pallas kernels for 0%

commit v1 on v0

--- a/solution.py
+++ b/solution.py
@@ -118,8 +118,13 @@
     )
     window_state = absorb_block(empty_state, window_scores, causal, fresh_values)
     occluded_flags = occluded.astype(jnp.bfloat16)
-    keys_block = lax.all_gather(cache_keys, "dp", axis=0, tiled=True)
-    values_block = lax.all_gather(cache_values, "dp", axis=0, tiled=True)
+    keys_block, values_block = jnp.split(
+        lax.all_gather(
+            jnp.concatenate([cache_keys, cache_values], axis=1), "dp", axis=0, tiled=True
+        ),
+        [cache_keys.shape[1]],
+        axis=1,
+    )
     flags_block = lax.all_gather(occluded_flags, "dp", axis=0, tiled=True)
     block_length = keys_block.shape[0]
     scores = (

time: 561 us -> 584 us (1.041)
  waiting for transfers between devices: 438 us -> 471 us
  blocking collectives: 42.4 us -> 30.8 us
    all_gather x2 -> x0, blocking collectives: 15 us -> none  [the longest x1 7.89 us: local(): keys_block = lax.all_gather(cache_keys, 'dp', axis=0, tiled=True)]
    reduce_scatter x1, waiting for transfers between devices: 14.3 us -> 28 us  [local(): lax.psum_scatter(jnp.dot(row_block, query_weight, preferred_element_type=...]
    all_gather x0 -> x1, waiting for transfers between devices: none -> 10.6 us  [local(): lax.all_gather(jnp.concatenate([cache_keys, cache_values], axis=1), 'dp',...]
    psum x1, waiting for transfers between devices: 0.02 us -> 9.82 us  [local(): lax.psum((jnp.dot(columns, key_weight, preferred_element_type=jnp.float32...]
  transfers between devices with their start and end apart: 8 -> 9, of which waited for: 7 -> 9; matrix products, arithmetic and copies ran while one was open for 2% -> 3% of each run, Pallas kernels for 0% -> 0%
where the time goes in v1:
time: 584 us
  waiting for transfers between devices  471 us (81%)
  matrix products  51.2 us (9%)
  blocking collectives  30.8 us (5%)
  between operations  13.5 us (2%)
  other arithmetic  12 us (2%)
    all_gather x1, waiting for transfers between devices, local(): lax.all_gather(out_weight, 'fsdp', axis=1, tiled=True)  145 us
    reduce_scatter x1, waiting for transfers between devices, local(): lax.psum_scatter(jnp.dot(row_block, down_rows, preferred_element_type=jnp...  85.5 us
    all_gather x1, waiting for transfers between devices, local(): piece_rows = lax.all_gather(send_rows, ('dp', 'fsdp'), axis=0, tiled=True)  73.7 us
    all_gather x1, waiting for transfers between devices, local(): everyone = lax.all_gather(normed, 'fsdp', axis=0, tiled=True)  47.5 us
    psum x1, waiting for transfers between devices, local(): mixture = lax.psum(returned * weight_mine[:, None], 'expert')  36 us
    psum x1, waiting for transfers between devices, local(): residual = window.astype(jnp.float32) + lax.psum(head_terms, 'expert')  34.1 us
    reduce_scatter x1, waiting for transfers between devices, local(): lax.psum_scatter(jnp.dot(row_block, query_weight, preferred_element_type=...  28 us
    psum x1, blocking collectives, local(): lax.psum((jnp.dot(columns, key_weight, preferred_element_type=jnp.float32...  26.4 us
  transfers between devices with their start and end apart: 9, of which 9 were waited for; matrix products, arithmetic and copies ran while one was open for 3% of the time, Pallas kernels for 0%

profile of v1, /device:TPU:0, one launch (start us, length us, event | category | flops | bytes accessed | tf_op | source)
XLA Modules:
  0.0 583.7 jit_solution(5739063835538089802)
XLA Ops:
  6.5 1.4 fusion.29
  8.0 2.1 fusion.31
  10.4 0.8 pad_maximum_fusion
  11.4 47.5 %all-gather.7.cloned.1.call-done = bf16[256,4096]{1,0:T(8,128)(2,1)} async-done(((bf16[64,4096]{1,0:T(8,128)(2,1)}), bf16[256,4096]{1,0:T(8,128)(2,1)}) %all-gather.7.cloned.1.call-update) | async-done | bytes 2097168 | tf_op jit(solution)/shard_map/all_gather | solution.py:80
  58.9 1.4 fusion.43
  60.3 0.9 copy.41
  61.2 2.7 fusion.45
  64.6 4.3 all_gather.15
  69.9 10.6 %all-gather.5.cloned.1.call-done = bf16[1024,512]{0,1:T(8,128)(2,1)} async-done(((bf16[512,512]{0,1:T(8,128)(2,1)}), bf16[1024,512]{0,1:T(8,128)(2,1)}) %all-gather.5.cloned.1.call-update) | async-done | bytes 1048592 | tf_op jit(solution)/shard_map/all_gather | solution.py:122
  80.5 1.3 fusion.79
  81.7 1.3 fusion.41
  83.1 26.4 %all-reduce.10 = bf16[256,256]{1,0:T(8,128)(2,1)S(1)} all-reduce(f32[256,256]{1,0:T(8,128)S(1)} %fusion.41), channel_id=1, replica_groups=mesh['dp'=2,'fsdp'=4,'expert'=4] {'fsdp'}, use_global_device_ids=true, to_apply=%region_5.6 | all-reduce | flops 65536 | bytes 393216 | tf_op jit(solution)/shard_map/psum | solution.py:90
  109.6 9.8 %all-reduce.5.cloned.1.call-done = f32[256,2,128]{2,0,1:T(8,128)} async-done(((f32[256,2,128]{2,0,1:T(8,128)}), f32[256,2,128]{2,0,1:T(8,128)}) %all-reduce.5.cloned.1.call-update) | async-done | bytes 262160 | tf_op jit(solution)/shard_map/psum | solution.py:90
  119.4 1.2 subtract_convert_fusion
  120.6 28.0 %reduce-scatter.3.cloned.1.call-done = f32[64,1024]{1,0:T(8,128)} async-done(((f32[256,1024]{1,0:T(8,128)}), f32[64,1024]{1,0:T(8,128)}) %reduce-scatter.3.cloned.1.call-update) | async-done | bytes 262160 | tf_op jit(solution)/shard_map/reduce_scatter | solution.py:84
  148.6 1.0 copy.55
  150.5 0.6 bitcast_reduce_fusion
  151.1 0.6 fusion.20
  151.8 0.6 fusion.27
  152.9 145.4 %all-gather.9.cloned.1.call-done = bf16[1024,4096]{1,0:T(8,128)(2,1)} async-done(((bf16[1024,1024]{1,0:T(8,128)(2,1)}), bf16[1024,4096]{1,0:T(8,128)(2,1)}) %all-gather.9.cloned.1.call-update) | async-done | bytes 8388624 | tf_op jit(solution)/shard_map/all_gather | solution.py:155
  298.3 6.0 %fusion.81 = f32[64,4096]{1,0:T(8,128)} fusion(bf16[64,1024]{1,0:T(8,128)(2,1)S(1)} %convert_element_type.96, bf16[1024,4096]{1,0:T(8,128)(2,1)} %all-gather.9.cloned.1.call-done), kind=kOutput, calls=%fused_computation.115 | convolution fusion | flops 536870912 | bytes 9568256 | tf_op jit(solution)/shard_map/dot_general | solution.py:153
  304.8 34.1 %all-reduce.7.cloned.1.call-done = f32[64,4096]{1,0:T(8,128)} async-done(((f32[64,4096]{1,0:T(8,128)}), f32[64,4096]{1,0:T(8,128)}) %all-reduce.7.cloned.1.call-update) | async-done | bytes 1048592 | tf_op jit(solution)/shard_map/psum | solution.py:158
  338.8 1.6 multiply_reduce_fusion
  340.6 1.2 convolution_convert_fusion
  342.1 73.7 %all-gather.11.cloned.1.call-done = bf16[512,4096]{1,0:T(8,128)(2,1)} async-done(((bf16[64,4096]{1,0:T(8,128)(2,1)}), bf16[512,4096]{1,0:T(8,128)(2,1)}) %all-gather.11.cloned.1.call-update) | async-done | bytes 4194320 | tf_op jit(solution)/shard_map/all_gather | solution.py:184
  415.8 12.2 %fusion.4 = f32[512,1536]{1,0:T(8,128)} fusion(bf16[512,4096]{1,0:T(8,128)(2,1)} %all-gather.11.cloned.1.call-done, bf16[1,1536,4096]{2,1,0:T(8,128)(2,1)} %param.27), kind=kOutput, calls=%fused_computation.4 | convolution fusion | flops 6442450944 | bytes 19922944 | tf_op jit(solution)/shard_map/dot_general | solution.py:185
  427.9 21.8 %fusion.6 = bf16[512,4096]{1,0:T(8,128)(2,1)} fusion(bf16[1,1536,4096]{2,1,0:T(8,128)(2,1)} %param.29, bf16[512,4096]{1,0:T(8,128)(2,1)} %all-gather.11.cloned.1.call-done, bf16[1,1536,4096]{2,1,0:T(8,128)(2,1)} %param.28, f32[512,1536]{1,0:T(8,128)} %fusion.4), kind=kOutput, calls=%fused_computation.6 | convolution fusion | flops 12891717632 | bytes 36700160 | tf_op jit(solution)/shard_map/dot_general | solution.py:192
  449.8 0.7 copy-done.8
  450.8 85.5 %reduce-scatter.5.cloned.1.call-done = bf16[64,4096]{1,0:T(8,128)(2,1)} async-done(((bf16[512,4096]{1,0:T(8,128)(2,1)}), bf16[64,4096]{1,0:T(8,128)(2,1)}) %reduce-scatter.5.cloned.1.call-update) | async-done | bytes 524304 | tf_op jit(solution)/shard_map/reduce_scatter | solution.py:191
  536.3 2.4 convolution_multiply_fusion
  538.7 36.0 %all-reduce.9.cloned.1.call-done = f32[64,4096]{1,0:T(8,128)} async-done(((f32[64,4096]{1,0:T(8,128)}), f32[64,4096]{1,0:T(8,128)}) %all-reduce.9.cloned.1.call-update) | async-done | bytes 1048592 | tf_op jit(solution)/shard_map/psum | solution.py:203
  574.7 2.5 fusion.38
  (77 shorter events, 4.7 us)
Async XLA Ops:
  6.5 54.7 %copy-start = (bf16[1024,1024]{1,0:T(8,128)(2,1)S(1)}, bf16[1024,1024]{1,0:T(8,128)(2,1)}, u32[]{:S(2)}) copy-start(bf16[1024,1024]{1,0:T(8,128)(2,1)} %param.17) | copy-start | bytes 6291460
  6.5 3.6 copy-start.6
  6.5 3.7 copy-start.7
  6.5 52.3 %all-gather.7.cloned.1.call-start = ((), (), s32[]{:S(2)}) async-start(), calls=%async_computation.3 | async-start | bytes 2621440 | tf_op jit(solution)/shard_map/all_gather | solution.py:80
  8.0 50.9 %copy-start.4 = (bf16[1024,256]{1,0:T(8,128)(2,1)S(1)}, bf16[1024,256]{1,0:T(8,128)(2,1)}, u32[]{:S(2)}) copy-start(bf16[1024,256]{1,0:T(8,128)(2,1)} %param.18) | copy-start | bytes 1572868
  10.1 70.4 %all-gather.5.cloned.1.call-start = ((), (), s32[]{:S(2)}) async-start(), calls=%async_computation.2 | async-start | bytes 1572864 | tf_op jit(solution)/shard_map/all_gather | solution.py:122
  11.3 108.1 %all-reduce.5.cloned.1.call-start = ((), (), s32[]{:S(2)}) async-start(), calls=%async_computation.5 | async-start | bytes 524288 | tf_op jit(solution)/shard_map/psum | solution.py:90
  61.1 87.4 %reduce-scatter.3.cloned.1.call-start = ((), (), s32[]{:S(2)}) async-start(), calls=%async_computation.4 | async-start | bytes 1310720 | tf_op jit(solution)/shard_map/reduce_scatter | solution.py:84
  63.9 0.7 copy-start.11
  64.0 17.8 %copy-start.5 = (bf16[1024,256]{1,0:T(8,128)(2,1)S(1)}, bf16[1024,256]{1,0:T(8,128)(2,1)}, u32[]{:S(2)}) copy-start(bf16[1024,256]{1,0:T(8,128)(2,1)} %param.19) | copy-start | bytes 1572868
  64.0 234.3 %all-gather.9.cloned.1.call-start = ((), (), s32[]{:S(2)}) async-start(), calls=%async_computation.6 | async-start | bytes 10485760 | tf_op jit(solution)/shard_map/all_gather | solution.py:155
  64.6 274.3 %all-reduce.7.cloned.1.call-start = ((), (), s32[]{:S(2)}) async-start(), calls=%async_computation.7 | async-start | bytes 2097152 | tf_op jit(solution)/shard_map/psum | solution.py:158
  152.9 151.5 %copy-start.10 = (s32[1,64,2]{1,2,0:T(2,128)S(1)}, s32[1,64,2]{1,2,0:T(2,128)}, u32[]{:S(2)}) copy-start(s32[1,64,2]{1,2,0:T(2,128)} %param.26) | copy-start | bytes 1540
  152.9 185.9 %copy-start.2 = (bf16[64,4096]{1,0:T(8,128)(2,1)S(1)}, bf16[64,4096]{1,0:T(8,128)(2,1)}, u32[]{:S(2)}) copy-start(bf16[64,4096]{1,0:T(8,128)(2,1)} %param.15) | copy-start | bytes 1572868
  304.3 36.1 %copy-start.9 = (f32[4096]{0:T(1024)S(1)}, f32[4096]{0:T(1024)}, u32[]{:S(2)}) copy-start(f32[4096]{0:T(1024)} %param.24) | copy-start | bytes 49156
  304.4 111.4 %all-gather.11.cloned.1.call-start = ((), (), s32[]{:S(2)}) async-start(), calls=%async_computation.8 | async-start | bytes 4718592 | tf_op jit(solution)/shard_map/all_gather | solution.py:184
  338.8 1.6 copy-start.3
  341.9 194.4 %reduce-scatter.5.cloned.1.call-start = ((), (), s32[]{:S(2)}) async-start(), calls=%async_computation.9 | async-start | bytes 4718592 | tf_op jit(solution)/shard_map/reduce_scatter | solution.py:191
  449.7 0.8 copy-start.8
  449.8 125.0 %all-reduce.9.cloned.1.call-start = ((), (), s32[]{:S(2)}) async-start(), calls=%async_computation.10 | async-start | bytes 2097152 | tf_op jit(solution)/shard_map/psum | solution.py:203
  538.7 38.5 %copy-start.1 = (bf16[1024,1024]{1,0:T(8,128)(2,1)S(1)}, bf16[1024,1024]{1,0:T(8,128)(2,1)}, u32[]{:S(2)}) copy-start(bf16[1024,1024]{1,0:T(8,128)(2,1)} %param.17) | copy-start | bytes 6291460
Sparse Core Ops, SparseCore 0:
  10.2 48.6 all-gather.6
  60.4 20.0 all-gather.4
  82.8 36.5 all-reduce.4
  121.7 26.8 reduce-scatter.2
  150.0 148.2 all-gather.8
  304.5 34.2 all-reduce.6
  342.0 73.7 all-gather.10
  449.9 86.3 reduce-scatter.4
  538.9 35.8 all-reduce.8
